TPU v7x, 32 devices: a whole 2x2x4 slice. The times are simulated.
32 devices in a mesh: ctx: 4 (over z), exp: 8 (over y, x, core).
Axes of the slice: x: 2, y: 2, z: 4, core: 2. Of those that a mesh axis runs over, the one named last changes fastest.
Arguments:
- out_grad: bfloat16 [4096, 2048], P(('ctx', 'exp')), may hold values from -6 to 6
- route_ids: int32 [4096, 4], P(('ctx', 'exp')), may hold values from 0 to 15, all different within a row; in each aligned block of 128 rows (0 to 127, 128 to 255, ...) at most 36 rows name the same one
- gate_probs: float32 [4096, 4], P(('ctx', 'exp')), may hold values from 0 to 1, as said below
- saved_hidden: bfloat16 [4, 8, 16, 36, 768], P('ctx', None, 'exp'), may hold values from -6 to 6
- down_weight: bfloat16 [16, 768, 2048], P('exp', None, 'ctx'), may hold values from -0.02734375 to 0.02734375
- router_weight: bfloat16 [2048, 16], replicated, may hold values from -1.5 to 1.5
- proj_weight: bfloat16 [4096, 2048], P('ctx'), may hold values from -0.125 to 0.125
Outputs:
- head_grads: bfloat16 [4, 1024, 4096], P(None, 'exp', 'ctx')
- router_grad: float32 [4096, 4], P(('ctx', 'exp'))
Inputs may be any that keep to these rules, and one draw needn't show every extreme that they name: `route_ids`: each token names 4 different experts; among the tokens of one device no expert is named more than 36 times, and in some device some expert is named exactly 36 times. `gate_probs`: positive; a token's 4 gates sum to one.
All inputs are finite; a program needn't handle non-finite values.
Results may differ from a plain program's by a relative error of at most 0.009.
Values may be sent and summed in bfloat16 or wider, within the bound.
A program may use at most 64 MiB of HBM per device.

v0:
```python
import jax
import jax.numpy as jnp
from jax import lax
from jax.sharding import PartitionSpec as P


def route_ranks(route_ids, experts):
    flat_ids = route_ids.reshape(-1)
    onehot = (flat_ids[:, None] == jnp.arange(experts, dtype=jnp.int32)[None, :]).astype(jnp.int32)
    earlier = jnp.cumsum(onehot, axis=0) - onehot
    slot_rank = jnp.sum(earlier * onehot, axis=1)
    return (flat_ids, slot_rank)


def shards(out_grad, route_ids, gate_probs, saved_hidden, down_weight, router_weight, proj_weight):
    tok_rows, top_count = route_ids.shape
    experts = router_weight.shape[1]
    groups = lax.axis_size("exp")
    n_ctx = lax.axis_size("ctx")
    local_experts = down_weight.shape[0]
    capacity = saved_hidden.shape[3]
    dslice = down_weight.shape[2]
    me_ctx = lax.axis_index("ctx")
    rows_all = lax.all_gather(out_grad, "ctx", axis=0, tiled=False)
    packed = jnp.concatenate([route_ids.astype(jnp.float32), gate_probs], axis=1)
    packed_all = lax.all_gather(packed, "ctx", axis=0, tiled=False)
    ids_all = packed_all[:, :, :top_count].astype(jnp.int32)
    probs_all = packed_all[:, :, top_count:]
    own = saved_hidden[0]
    right, left, from_left, from_right = (own, own, [], [])
    for _ in range(n_ctx - 1):
        right = lax.ppermute(right, "ctx", [(i, i + 1) for i in range(n_ctx - 1)])
        left = lax.ppermute(left, "ctx", [(i + 1, i) for i in range(n_ctx - 1)])
        from_left.append(right)
        from_right.append(left)
    hidden_all = jnp.zeros((n_ctx,) + own.shape, own.dtype)
    for k in range(n_ctx - 1, 0, -1):
        hidden_all = lax.dynamic_update_index_in_dim(
            hidden_all, from_left[k - 1], jnp.maximum(me_ctx - k, 0), 0
        )
    for k in range(n_ctx - 1, 0, -1):
        hidden_all = lax.dynamic_update_index_in_dim(
            hidden_all, from_right[k - 1], jnp.minimum(me_ctx + k, n_ctx - 1), 0
        )
    hidden_all = lax.dynamic_update_index_in_dim(hidden_all, own, me_ctx, 0)
    flat_ids, slot_rank = jax.vmap(lambda r: route_ranks(r, experts))(ids_all)
    positions = flat_ids * capacity + slot_rank
    cols = lax.dynamic_slice_in_dim(rows_all, me_ctx * dslice, dslice, axis=2)
    spread = jnp.repeat(cols, top_count, axis=1)
    blk = jnp.broadcast_to(jnp.arange(n_ctx, dtype=jnp.int32)[:, None], flat_ids.shape)
    send_rows = (
        jnp.zeros((groups, n_ctx, local_experts, capacity, dslice), out_grad.dtype)
        .at[flat_ids // local_experts, blk, flat_ids % local_experts, slot_rank]
        .set(spread)
    )
    arrived = lax.all_to_all(send_rows, "exp", split_axis=0, concat_axis=0, tiled=True)
    outputs = jnp.einsum(
        "csekf,efn->scekn", hidden_all, down_weight, preferred_element_type=jnp.float32
    ).astype(jnp.bfloat16)
    partial_grad = jnp.sum(arrived.astype(jnp.float32) * outputs.astype(jnp.float32), axis=4)
    returned = lax.all_to_all(partial_grad, "exp", split_axis=0, concat_axis=0, tiled=True)
    returned = lax.psum(returned, "ctx")
    returned = jnp.transpose(returned, (1, 0, 2, 3)).reshape(n_ctx, experts * capacity)
    picks = positions[:, :, None] == jnp.arange(experts * capacity, dtype=jnp.int32)[None, None, :]
    gate_grad = jnp.sum(jnp.where(picks, returned[:, None, :], 0.0), axis=2)
    gate_grad = gate_grad.reshape(n_ctx, tok_rows, top_count)
    weighted = jnp.sum(probs_all * gate_grad, axis=2, keepdims=True)
    router_all = probs_all * (gate_grad - weighted)
    matches = ids_all[:, :, :, None] == jnp.arange(experts, dtype=jnp.int32)[None, None, None, :]
    dense_all = jnp.sum(jnp.where(matches, router_all[:, :, :, None], 0.0), axis=2)
    router_wide = router_weight.astype(jnp.float32)
    combined = (
        rows_all.astype(jnp.float32)
        + lax.dot_general(
            dense_all, router_wide, (((2,), (1,)), ((), ())), precision=lax.Precision.HIGHEST
        )
    ).astype(jnp.bfloat16)
    head_flat = lax.dot_general(
        combined.reshape(n_ctx * tok_rows, -1),
        proj_weight,
        (((1,), (1,)), ((), ())),
        preferred_element_type=jnp.float32,
    ).astype(jnp.bfloat16)
    head_grads = head_flat.reshape(n_ctx, tok_rows, proj_weight.shape[0])
    router_grad = lax.dynamic_index_in_dim(router_all, me_ctx, axis=0, keepdims=False)
    return (head_grads, router_grad)


def solution(mesh):
    return jax.shard_map(
        shards,
        mesh=mesh,
        in_specs=(
            P(("ctx", "exp"), None),
            P(("ctx", "exp"), None),
            P(("ctx", "exp"), None),
            P("ctx", None, "exp", None, None),
            P("exp", None, "ctx"),
            P(),
            P("ctx", None),
        ),
        out_specs=(P(None, "exp", "ctx"), P(("ctx", "exp"), None)),
        check_vma=False,
    )
```

profile of v0, /device:TPU:0, one launch (start us, length us, event | category | flops | bytes accessed | tf_op | source)
XLA Modules:
  0.0 219.9 jit_solution(10738357573883738285)
XLA Ops:
  7.9 5.9 %collective-permute-start = (bf16[8,2,36,768]{3,1,2,0:T(2,128)(2,1)}, bf16[8,2,36,768]{3,1,2,0:T(2,128)(2,1)}, u32[]{:S(2)}, u32[]{:S(2)}) collective-permute-start(bf16[8,2,36,768]{3,1,2,0:T(2,128)(2,1)} %bitcast.61), channel_id=1, source_target_pairs={{0,8},{8,16},{16,24},{1,9},{9,17},{17,25},{2,10},{10,18},{18,26},{... | collective-permute-start | bytes 2654216 | tf_op jit(solution)/shard_map/ppermute | solution.py:32
  15.1 29.6 %collective-permute-done = bf16[8,2,36,768]{3,1,2,0:T(2,128)(2,1)} collective-permute-done((bf16[8,2,36,768]{3,1,2,0:T(2,128)(2,1)}, bf16[8,2,36,768]{3,1,2,0:T(2,128)(2,1)}, u32[]{:S(2)}, u32[]{:S(2)}) %collective-permute-start) | collective-permute-done | bytes 884768 | tf_op jit(solution)/shard_map/ppermute | solution.py:32
  44.6 15.3 %collective-permute-start.1 = (bf16[8,2,36,768]{3,1,2,0:T(2,128)(2,1)}, bf16[8,2,36,768]{3,1,2,0:T(2,128)(2,1)}, u32[]{:S(2)}, u32[]{:S(2)}) collective-permute-start(bf16[8,2,36,768]{3,1,2,0:T(2,128)(2,1)} %collective-permute-done), channel_id=1, source_target_pairs={{0,8},{8,16},{16,24},{1,9},{9,17},{17,25},{2,10},{10,18},{18,26},{... | collective-permute-start | bytes 2654216 | tf_op jit(solution)/shard_map/ppermute | solution.py:32
  61.3 31.7 %all-gather.1 = f32[512,8]{0,1:T(8,128)S(1)} all-gather(f32[128,8]{0,1:T(8,128)S(1)} %pad_maximum_fusion), channel_id=3, replica_groups=mesh['ctx'=4,'exp'=8] {'ctx'}, dimensions={0}, use_global_device_ids=true | all-gather | bytes 20480 | tf_op jit(solution)/shard_map/all_gather | solution.py:26
  93.8 4.6 %reduce-window.6 = s32[4,16,4,128]{3,1,2,0:T(8,128)S(1)} reduce-window(s32[4,16,4,128]{3,1,2,0:T(8,128)S(1)} %fusion.7, s32[]{:T(128)} %constant.71.clone.1), window={size=1x1x1x128 pad=0_0x0_0x0_0x127_0}, to_apply=%region_0.1 | reduce-window | flops 4161536 | bytes 262148 | tf_op jit(solution)/shard_map/reduce-window
  100.3 5.5 %collective-permute-start.2 = (bf16[8,2,36,768]{3,1,2,0:T(2,128)(2,1)}, bf16[8,2,36,768]{3,1,2,0:T(2,128)(2,1)}, u32[]{:S(2)}, u32[]{:S(2)}) collective-permute-start(bf16[8,2,36,768]{3,1,2,0:T(2,128)(2,1)} %collective-permute-done.1), channel_id=1, source_target_pairs={{0,8},{8,16},{16,24},{1,9},{9,17},{17,25},{2,10},{10,18},{18,26},{... | collective-permute-start | bytes 2654216 | tf_op jit(solution)/shard_map/ppermute | solution.py:32
  110.3 4.0 %reshape.204 = bf16[2048,512]{1,0:T(8,128)(2,1)} reshape(bf16[4,128,4,512]{3,2,1,0:T(4,128)(2,1)} %broadcast_in_dim.74) | data formatting | bytes 4194304 | tf_op jit(solution)/shard_map/reshape | solution.py:49
  114.3 11.6 %scatter_custom_fusion = bf16[2304,512]{1,0:T(8,128)(2,1)} fusion(s32[2048]{0:T(1024)S(1)} %bitcast.65, bf16[2048,512]{1,0:T(8,128)(2,1)} %reshape.204, bf16[]{:T(256)} %constant.72.clone.1), kind=kCustom, calls=%fused_computation.8 | custom fusion | bytes 2359808
  125.9 5.9 %reshape.200 = bf16[8,4,36,2,512]{4,3,2,1,0:T(2,128)(2,1)} reshape(bf16[2304,512]{1,0:T(8,128)(2,1)} %scatter_custom_fusion) | data formatting | bytes 4718592
  131.8 4.3 %copy.69 = bf16[8,4,2,36,512]{4,1,3,2,0:T(4,128)(2,1)} copy(bf16[8,4,2,36,512]{4,2,3,1,0:T(2,128)(2,1)} %bitcast.54) | data formatting | bytes 4718592 | tf_op jit(solution)/shard_map/scatter | solution.py:54
  136.1 4.4 %all-to-all-start = ((bf16[8,4,2,36,512]{4,1,3,2,0:T(4,128)(2,1)}), bf16[8,4,2,36,512]{4,1,3,2,0:T(4,128)(2,1)}, u32[]{:S(2)}, u32[]{:S(2)}) async-start(bf16[8,4,2,36,512]{4,1,3,2,0:T(4,128)(2,1)} %copy.69), calls=%async_computation | async-start | bytes 4718592 | tf_op jit(solution)/shard_map/all_to_all | solution.py:56
  142.0 2.1 broadcast_in_dim.75
  144.2 2.2 %copy_dynamic-update-slice_fusion.6 = bf16[4,8,2,36,768]{4,3,1,0,2:T(8,128)(2,1)} fusion(bf16[4,8,2,36,768]{4,3,1,0,2:T(8,128)(2,1)} %broadcast_in_dim.75, s32[]{:T(128)S(6)} %max.9, bf16[1,8,2,36,768]{4,2,3,1,0:T(2,128)(2,1)} %bitcast.6), kind=kLoop, calls=%fused_computation.16 | loop fusion | bytes 1867780 | tf_op jit(solution)/shard_map/jit(dynamic_update_index_in_dim)/dynamic_update_slice | solution.py:38
  146.4 2.2 %copy_dynamic-update-slice_fusion.5 = bf16[4,8,2,36,768]{4,3,1,0,2:T(8,128)(2,1)} fusion(bf16[4,8,2,36,768]{4,3,1,0,2:T(8,128)(2,1)} %copy_dynamic-update-slice_fusion.6, s32[]{:T(128)S(6)} %max.10, bf16[1,8,2,36,768]{4,2,3,1,0:T(2,128)(2,1)} %bitcast.7), kind=kLoop, calls=%fused_computation.15 | loop fusion | bytes 1867780 | tf_op jit(solution)/shard_map/jit(dynamic_update_index_in_dim)/dynamic_update_slice | solution.py:38
  148.6 2.3 %copy_dynamic-update-slice_fusion.4 = bf16[4,8,2,36,768]{4,3,1,0,2:T(8,128)(2,1)} fusion(bf16[4,8,2,36,768]{4,3,1,0,2:T(8,128)(2,1)} %copy_dynamic-update-slice_fusion.5, s32[]{:T(128)S(6)} %max.11, bf16[1,8,2,36,768]{4,2,3,1,0:T(2,128)(2,1)} %bitcast.8), kind=kLoop, calls=%fused_computation.14 | loop fusion | bytes 1867780 | tf_op jit(solution)/shard_map/jit(dynamic_update_index_in_dim)/dynamic_update_slice | solution.py:38
  151.0 13.7 %collective-permute-done.5 = bf16[8,2,36,768]{3,1,2,0:T(2,128)(2,1)} collective-permute-done((bf16[8,2,36,768]{3,1,2,0:T(2,128)(2,1)}, bf16[8,2,36,768]{3,1,2,0:T(2,128)(2,1)}, u32[]{:S(2)}, u32[]{:S(2)}) %collective-permute-start.5) | collective-permute-done | bytes 884768 | tf_op jit(solution)/shard_map/ppermute | solution.py:33
  164.7 2.2 %copy_dynamic-update-slice_fusion.3 = bf16[4,8,2,36,768]{4,3,1,0,2:T(8,128)(2,1)} fusion(bf16[4,8,2,36,768]{4,3,1,0,2:T(8,128)(2,1)} %copy_dynamic-update-slice_fusion.4, s32[]{:T(128)S(6)} %select_n.93, bf16[1,8,2,36,768]{4,2,3,1,0:T(2,128)(2,1)} %bitcast.9), kind=kLoop, calls=%fused_computation.13 | loop fusion | bytes 1867780 | tf_op jit(solution)/shard_map/jit(dynamic_update_index_in_dim)/dynamic_update_slice | solution.py:42
  166.9 2.2 %copy_dynamic-update-slice_fusion.2 = bf16[4,8,2,36,768]{4,3,1,0,2:T(8,128)(2,1)} fusion(bf16[4,8,2,36,768]{4,3,1,0,2:T(8,128)(2,1)} %copy_dynamic-update-slice_fusion.3, s32[]{:T(128)S(6)} %select_n.94, bf16[1,8,2,36,768]{4,2,3,1,0:T(2,128)(2,1)} %bitcast.10), kind=kLoop, calls=%fused_computation.12 | loop fusion | bytes 1867780 | tf_op jit(solution)/shard_map/jit(dynamic_update_index_in_dim)/dynamic_update_slice | solution.py:42
  171.3 5.6 %fusion = f32[8,4,2,36]{3,0,1,2:T(8,128)S(1)} fusion(bf16[8,4,2,36,512]{4,1,3,2,0:T(4,128)(2,1)} %all-to-all-done, bf16[4,8,2,36,768]{4,3,1,0,2:T(8,128)(2,1)} %copy_dynamic-update-slice_fusion, bf16[2,768,512]{2,1,0:T(8,128)(2,1)S(1)} %copy-done), kind=kOutput, calls=%fused_computation.2 | convolution fusion | flops 1817835264 | bytes 7480320 | tf_op jit(solution)/shard_map/csekf,efn->scekn/dot_general | solution.py:57
  177.6 3.8 %all-to-all-start.1 = ((f32[8,1,288]{2,1,0:T(1,128)}), f32[8,1,288]{2,1,0:T(1,128)S(1)}, u32[]{:S(2)}, u32[]{:S(2)}) async-start(f32[8,1,288]{2,1,0:T(1,128)} %reshape.216), calls=%async_computation.1 | async-start | bytes 24576 | tf_op jit(solution)/shard_map/all_to_all | solution.py:61
  181.6 4.6 %all-to-all-done.1 = f32[8,1,288]{2,1,0:T(1,128)S(1)} async-done(((f32[8,1,288]{2,1,0:T(1,128)}), f32[8,1,288]{2,1,0:T(1,128)S(1)}, u32[]{:S(2)}, u32[]{:S(2)}) %all-to-all-start.1) | async-done | bytes 9248 | tf_op jit(solution)/shard_map/all_to_all | solution.py:61
  187.6 16.1 %psum.7 = f32[4,576]{1,0:T(4,128)S(1)} all-reduce(f32[4,576]{1,0:T(4,128)S(1)} %broadcast_in_dim.82), channel_id=1, replica_groups=mesh['ctx'=4,'exp'=8] {'ctx'}, use_global_device_ids=true, to_apply=%region_5.6 | all-reduce | flops 2304 | bytes 18432 | tf_op jit(solution)/shard_map/psum | solution.py:62
  206.0 3.7 %add_convert_fusion = bf16[4,128,2048]{2,1,0:T(8,128)(2,1)S(1)} fusion(bf16[4,128,2048]{2,1,0:T(8,128)(2,1)} %bitcast.59, f32[4,128,16]{1,2,0:T(8,128)S(1)} %select_reduce_fusion.1, bf16[2048,16]{0,1:T(8,128)(2,1)S(1)} %copy-done.2), kind=kOutput, calls=%fused_computation.5 | convolution fusion | flops 204472320 | bytes 4292608 | tf_op jit(solution)/shard_map/dot_general | solution.py:74
  209.7 3.3 %convolution_convert_fusion = bf16[512,1024]{1,0:T(8,128)(2,1)} fusion(bf16[512,2048]{1,0:T(8,128)(2,1)S(1)} %bitcast.60, bf16[1024,2048]{1,0:T(8,128)(2,1)S(1)} %copy-done.3), kind=kOutput, calls=%fused_computation.7 | convolution fusion | flops 2148007936 | bytes 7340032 | tf_op jit(solution)/shard_map/dot_general | solution.py:78
  (58 shorter events, 18.6 us)
Async XLA Ops:
  7.2 164.1 %copy-start = (bf16[2,768,512]{2,1,0:T(8,128)(2,1)S(1)}, bf16[2,768,512]{2,1,0:T(8,128)(2,1)}, u32[]{:S(2)}) copy-start(bf16[2,768,512]{2,1,0:T(8,128)(2,1)} %param.11) | copy-start | bytes 4718596
  7.2 100.1 %all-gather.4.cloned.1.call-start = ((), (), s32[]{:S(2)}) async-start(), calls=%async_computation.2 | async-start | bytes 2621440 | tf_op jit(solution)/shard_map/all_gather | solution.py:24
  7.9 36.7 %collective-permute-start = (bf16[8,2,36,768]{3,1,2,0:T(2,128)(2,1)}, bf16[8,2,36,768]{3,1,2,0:T(2,128)(2,1)}, u32[]{:S(2)}, u32[]{:S(2)}) collective-permute-start(bf16[8,2,36,768]{3,1,2,0:T(2,128)(2,1)} %bitcast.61), channel_id=1, source_target_pairs={{0,8},{8,16},{16,24},{1,9},{9,17},{17,25},{2,10},{10,18},{18,26},{... | collective-permute-start | bytes 2654216 | tf_op jit(solution)/shard_map/ppermute | solution.py:32
  13.8 85.1 %collective-permute-start.3 = (bf16[8,2,36,768]{3,1,2,0:T(2,128)(2,1)}, bf16[8,2,36,768]{3,1,2,0:T(2,128)(2,1)S(1)}, u32[]{:S(2)}, u32[]{:S(2)}) collective-permute-start(bf16[8,2,36,768]{3,1,2,0:T(2,128)(2,1)} %bitcast.62), channel_id=1, source_target_pairs={{8,0},{16,8},{24,16},{9,1},{17,9},{25,17},{10,2},{18,10},{26,18},{... | collective-permute-start | bytes 2654216 | tf_op jit(solution)/shard_map/ppermute | solution.py:33
  44.6 55.6 %collective-permute-start.1 = (bf16[8,2,36,768]{3,1,2,0:T(2,128)(2,1)}, bf16[8,2,36,768]{3,1,2,0:T(2,128)(2,1)}, u32[]{:S(2)}, u32[]{:S(2)}) collective-permute-start(bf16[8,2,36,768]{3,1,2,0:T(2,128)(2,1)} %collective-permute-done), channel_id=1, source_target_pairs={{0,8},{8,16},{16,24},{1,9},{9,17},{17,25},{2,10},{10,18},{18,26},{... | collective-permute-start | bytes 2654216 | tf_op jit(solution)/shard_map/ppermute | solution.py:32
  99.0 41.6 %collective-permute-start.4 = (bf16[8,2,36,768]{3,1,2,0:T(2,128)(2,1)S(1)}, bf16[8,2,36,768]{3,1,2,0:T(2,128)(2,1)}, u32[]{:S(2)}, u32[]{:S(2)}) collective-permute-start(bf16[8,2,36,768]{3,1,2,0:T(2,128)(2,1)S(1)} %collective-permute-done.3), channel_id=1, source_target_pairs={{8,0},{16,8},{24,16},{9,1},{17,9},{25,17},{10,2},{18,10},{26,18},{... | collective-permute-start | bytes 2654216 | tf_op jit(solution)/shard_map/ppermute | solution.py:33
  100.3 41.8 %collective-permute-start.2 = (bf16[8,2,36,768]{3,1,2,0:T(2,128)(2,1)}, bf16[8,2,36,768]{3,1,2,0:T(2,128)(2,1)}, u32[]{:S(2)}, u32[]{:S(2)}) collective-permute-start(bf16[8,2,36,768]{3,1,2,0:T(2,128)(2,1)} %collective-permute-done.1), channel_id=1, source_target_pairs={{0,8},{8,16},{16,24},{1,9},{9,17},{17,25},{2,10},{10,18},{18,26},{... | collective-permute-start | bytes 2654216 | tf_op jit(solution)/shard_map/ppermute | solution.py:32
  136.1 35.1 %all-to-all-start = ((bf16[8,4,2,36,512]{4,1,3,2,0:T(4,128)(2,1)}), bf16[8,4,2,36,512]{4,1,3,2,0:T(4,128)(2,1)}, u32[]{:S(2)}, u32[]{:S(2)}) async-start(bf16[8,4,2,36,512]{4,1,3,2,0:T(4,128)(2,1)} %copy.69), calls=%async_computation | async-start | bytes 4718592 | tf_op jit(solution)/shard_map/all_to_all | solution.py:56
  140.5 24.1 %collective-permute-start.5 = (bf16[8,2,36,768]{3,1,2,0:T(2,128)(2,1)}, bf16[8,2,36,768]{3,1,2,0:T(2,128)(2,1)}, u32[]{:S(2)}, u32[]{:S(2)}) collective-permute-start(bf16[8,2,36,768]{3,1,2,0:T(2,128)(2,1)} %collective-permute-done.4), channel_id=1, source_target_pairs={{8,0},{16,8},{24,16},{9,1},{17,9},{25,17},{10,2},{18,10},{26,18},{... | collective-permute-start | bytes 2654216 | tf_op jit(solution)/shard_map/ppermute | solution.py:33
  148.6 21.5 %copy-start.1 = (bf16[1,8,2,36,768]{4,2,3,1,0:T(2,128)(2,1)S(1)}, bf16[1,8,2,36,768]{4,2,3,1,0:T(2,128)(2,1)}, u32[]{:S(2)}) copy-start(bf16[1,8,2,36,768]{4,2,3,1,0:T(2,128)(2,1)} %param.10) | copy-start | bytes 2654212
  171.2 34.7 %copy-start.2 = (bf16[2048,16]{0,1:T(8,128)(2,1)S(1)}, bf16[2048,16]{0,1:T(8,128)(2,1)}, u32[]{:S(2)}) copy-start(bf16[2048,16]{0,1:T(8,128)(2,1)} %param.12) | copy-start | bytes 196612
  177.6 8.6 %all-to-all-start.1 = ((f32[8,1,288]{2,1,0:T(1,128)}), f32[8,1,288]{2,1,0:T(1,128)S(1)}, u32[]{:S(2)}, u32[]{:S(2)}) async-start(f32[8,1,288]{2,1,0:T(1,128)} %reshape.216), calls=%async_computation.1 | async-start | bytes 24576 | tf_op jit(solution)/shard_map/all_to_all | solution.py:61
  206.0 3.7 %copy-start.3 = (bf16[1024,2048]{1,0:T(8,128)(2,1)S(1)}, bf16[1024,2048]{1,0:T(8,128)(2,1)}, u32[]{:S(2)}) copy-start(bf16[1024,2048]{1,0:T(8,128)(2,1)} %param.13) | copy-start | bytes 12582916
Sparse Core Ops, SparseCore 0:
  9.6 66.6 all-gather.3
where the time goes:
time: 221 us; the launch traced here: 220 us
  waiting for transfers between devices  48.6 us (22%)
  local copies, waits for them, and re-layouts  48 us (22%)
  blocking collectives  47.8 us (22%)
  starting transfers between devices  39 us (18%)
  between operations  14.3 us (6%)
  matrix products  12.6 us (6%)
  other arithmetic  9.51 us (4%)
    all_gather x1, blocking collectives, shards(): packed_all = lax.all_gather(packed, 'ctx', axis=0, tiled=False)  31.7 us
    ppermute x3, waiting for transfers between devices, shards(): right = lax.ppermute(right, 'ctx', [(i, i + 1) for i in range(n_ctx - 1)])  29.6 us
    ppermute x3, starting transfers between devices, shards(): right = lax.ppermute(right, 'ctx', [(i, i + 1) for i in range(n_ctx - 1)])  26.7 us
    unnamed x13, local copies, waits for them, and re-layouts  18.4 us
    psum x1, blocking collectives, shards(): returned = lax.psum(returned, 'ctx')  16.1 us
    ppermute x3, waiting for transfers between devices, shards(): left = lax.ppermute(left, 'ctx', [(i + 1, i) for i in range(n_ctx - 1)])  13.7 us
    dynamic_update_slice x3, local copies, waits for them, and re-layouts, shards(): lax.dynamic_update_index_in_dim(hidden_all, from_left[k - 1], jnp.maximum...  6.78 us
    dot_general x1, matrix products, shards(): jnp.einsum('csekf,efn->scekn', hidden_all, down_weight, preferred_element...  5.59 us
  transfers between devices with their start and end apart: 9, of which 3 were waited for; matrix products, arithmetic and copies ran while one was open for 24% of the time, Pallas kernels for 0%

commit v1 on v0

--- a/solution.py
+++ b/solution.py
@@ -59,7 +59,12 @@
     ).astype(jnp.bfloat16)
     partial_grad = jnp.sum(arrived.astype(jnp.float32) * outputs.astype(jnp.float32), axis=4)
     returned = lax.all_to_all(partial_grad, "exp", split_axis=0, concat_axis=0, tiled=True)
-    returned = lax.psum(returned, "ctx")
+
+    def tell_scenes(a0):
+        part_next = lax.all_gather(a0, axis_name="ctx")
+        return jnp.sum(part_next, 0)
+
+    returned = tell_scenes(returned)
     returned = jnp.transpose(returned, (1, 0, 2, 3)).reshape(n_ctx, experts * capacity)
     picks = positions[:, :, None] == jnp.arange(experts * capacity, dtype=jnp.int32)[None, None, :]
     gate_grad = jnp.sum(jnp.where(picks, returned[:, None, :], 0.0), axis=2)

time: 221 us -> 218 us (0.986)
  blocking collectives: 47.8 us -> 45.1 us
    psum x1 -> x0, blocking collectives: 16.1 us -> none  [shards(): returned = lax.psum(returned, 'ctx')]
    all_gather x0 -> x1, blocking collectives: none -> 13.4 us  [tell_scenes(): part_next = lax.all_gather(a0, axis_name='ctx')]
where the time goes in v1:
time: 218 us; the launch traced here: 217 us
  waiting for transfers between devices  48.6 us (22%)
  local copies, waits for them, and re-layouts  48 us (22%)
  blocking collectives  45.1 us (21%)
  starting transfers between devices  39 us (18%)
  between operations  14.3 us (7%)
  matrix products  12.6 us (6%)
  other arithmetic  9.55 us (4%)
    all_gather x1, blocking collectives, shards(): packed_all = lax.all_gather(packed, 'ctx', axis=0, tiled=False)  31.7 us
    ppermute x3, waiting for transfers between devices, shards(): right = lax.ppermute(right, 'ctx', [(i, i + 1) for i in range(n_ctx - 1)])  29.6 us
    ppermute x3, starting transfers between devices, shards(): right = lax.ppermute(right, 'ctx', [(i, i + 1) for i in range(n_ctx - 1)])  26.7 us
    unnamed x13, local copies, waits for them, and re-layouts  18.4 us
    ppermute x3, waiting for transfers between devices, shards(): left = lax.ppermute(left, 'ctx', [(i + 1, i) for i in range(n_ctx - 1)])  13.7 us
    all_gather x1, blocking collectives, tell_scenes(): part_next = lax.all_gather(a0, axis_name='ctx')  13.4 us
    dynamic_update_slice x3, local copies, waits for them, and re-layouts, shards(): lax.dynamic_update_index_in_dim(hidden_all, from_left[k - 1], jnp.maximum...  6.78 us
    dot_general x1, matrix products, shards(): jnp.einsum('csekf,efn->scekn', hidden_all, down_weight, preferred_element...  5.59 us
  transfers between devices with their start and end apart: 9, of which 3 were waited for; matrix products, arithmetic and copies ran while one was open for 24% of the time, Pallas kernels for 0%

profile of v1, /device:TPU:0, one launch (start us, length us, event | category | flops | bytes accessed | tf_op | source)
XLA Modules:
  0.0 217.2 jit_solution(12404448526780112093)
XLA Ops:
  7.9 5.9 %collective-permute-start = (bf16[8,2,36,768]{3,1,2,0:T(2,128)(2,1)}, bf16[8,2,36,768]{3,1,2,0:T(2,128)(2,1)}, u32[]{:S(2)}, u32[]{:S(2)}) collective-permute-start(bf16[8,2,36,768]{3,1,2,0:T(2,128)(2,1)} %bitcast.66), channel_id=1, source_target_pairs={{0,8},{8,16},{16,24},{1,9},{9,17},{17,25},{2,10},{10,18},{18,26},{... | collective-permute-start | bytes 2654216 | tf_op jit(solution)/shard_map/ppermute | solution.py:32
  15.1 29.6 %collective-permute-done = bf16[8,2,36,768]{3,1,2,0:T(2,128)(2,1)} collective-permute-done((bf16[8,2,36,768]{3,1,2,0:T(2,128)(2,1)}, bf16[8,2,36,768]{3,1,2,0:T(2,128)(2,1)}, u32[]{:S(2)}, u32[]{:S(2)}) %collective-permute-start) | collective-permute-done | bytes 884768 | tf_op jit(solution)/shard_map/ppermute | solution.py:32
  44.6 15.3 %collective-permute-start.1 = (bf16[8,2,36,768]{3,1,2,0:T(2,128)(2,1)}, bf16[8,2,36,768]{3,1,2,0:T(2,128)(2,1)}, u32[]{:S(2)}, u32[]{:S(2)}) collective-permute-start(bf16[8,2,36,768]{3,1,2,0:T(2,128)(2,1)} %collective-permute-done), channel_id=1, source_target_pairs={{0,8},{8,16},{16,24},{1,9},{9,17},{17,25},{2,10},{10,18},{18,26},{... | collective-permute-start | bytes 2654216 | tf_op jit(solution)/shard_map/ppermute | solution.py:32
  61.3 31.7 %all-gather.1 = f32[512,8]{0,1:T(8,128)S(1)} all-gather(f32[128,8]{0,1:T(8,128)S(1)} %pad_maximum_fusion), channel_id=3, replica_groups=mesh['ctx'=4,'exp'=8] {'ctx'}, dimensions={0}, use_global_device_ids=true | all-gather | bytes 20480 | tf_op jit(solution)/shard_map/all_gather | solution.py:26
  93.8 4.6 %reduce-window.6 = s32[4,16,4,128]{3,1,2,0:T(8,128)S(1)} reduce-window(s32[4,16,4,128]{3,1,2,0:T(8,128)S(1)} %fusion.7, s32[]{:T(128)} %constant.71.clone.1), window={size=1x1x1x128 pad=0_0x0_0x0_0x127_0}, to_apply=%region_0.1 | reduce-window | flops 4161536 | bytes 262148 | tf_op jit(solution)/shard_map/reduce-window
  100.3 5.5 %collective-permute-start.2 = (bf16[8,2,36,768]{3,1,2,0:T(2,128)(2,1)}, bf16[8,2,36,768]{3,1,2,0:T(2,128)(2,1)}, u32[]{:S(2)}, u32[]{:S(2)}) collective-permute-start(bf16[8,2,36,768]{3,1,2,0:T(2,128)(2,1)} %collective-permute-done.1), channel_id=1, source_target_pairs={{0,8},{8,16},{16,24},{1,9},{9,17},{17,25},{2,10},{10,18},{18,26},{... | collective-permute-start | bytes 2654216 | tf_op jit(solution)/shard_map/ppermute | solution.py:32
  110.3 4.0 %reshape.204 = bf16[2048,512]{1,0:T(8,128)(2,1)} reshape(bf16[4,128,4,512]{3,2,1,0:T(4,128)(2,1)} %broadcast_in_dim.74) | data formatting | bytes 4194304 | tf_op jit(solution)/shard_map/reshape | solution.py:49
  114.3 11.6 %scatter_custom_fusion = bf16[2304,512]{1,0:T(8,128)(2,1)} fusion(s32[2048]{0:T(1024)S(1)} %bitcast.73, bf16[2048,512]{1,0:T(8,128)(2,1)} %reshape.204, bf16[]{:T(256)} %constant.72.clone.1), kind=kCustom, calls=%fused_computation.8 | custom fusion | bytes 2359808
  125.9 5.9 %reshape.200 = bf16[8,4,36,2,512]{4,3,2,1,0:T(2,128)(2,1)} reshape(bf16[2304,512]{1,0:T(8,128)(2,1)} %scatter_custom_fusion) | data formatting | bytes 4718592
  131.8 4.3 %copy.82 = bf16[8,4,2,36,512]{4,1,3,2,0:T(4,128)(2,1)} copy(bf16[8,4,2,36,512]{4,2,3,1,0:T(2,128)(2,1)} %bitcast.59) | data formatting | bytes 4718592 | tf_op jit(solution)/shard_map/scatter | solution.py:54
  136.1 4.4 %all-to-all-start = ((bf16[8,4,2,36,512]{4,1,3,2,0:T(4,128)(2,1)}), bf16[8,4,2,36,512]{4,1,3,2,0:T(4,128)(2,1)}, u32[]{:S(2)}, u32[]{:S(2)}) async-start(bf16[8,4,2,36,512]{4,1,3,2,0:T(4,128)(2,1)} %copy.82), calls=%async_computation | async-start | bytes 4718592 | tf_op jit(solution)/shard_map/all_to_all | solution.py:56
  142.0 2.1 broadcast_in_dim.75
  144.2 2.2 %copy_dynamic-update-slice_fusion.6 = bf16[4,8,2,36,768]{4,3,1,0,2:T(8,128)(2,1)} fusion(bf16[4,8,2,36,768]{4,3,1,0,2:T(8,128)(2,1)} %broadcast_in_dim.75, s32[]{:T(128)S(6)} %max.9, bf16[1,8,2,36,768]{4,2,3,1,0:T(2,128)(2,1)} %bitcast.6), kind=kLoop, calls=%fused_computation.16 | loop fusion | bytes 1867780 | tf_op jit(solution)/shard_map/jit(dynamic_update_index_in_dim)/dynamic_update_slice | solution.py:38
  146.4 2.2 %copy_dynamic-update-slice_fusion.5 = bf16[4,8,2,36,768]{4,3,1,0,2:T(8,128)(2,1)} fusion(bf16[4,8,2,36,768]{4,3,1,0,2:T(8,128)(2,1)} %copy_dynamic-update-slice_fusion.6, s32[]{:T(128)S(6)} %max.10, bf16[1,8,2,36,768]{4,2,3,1,0:T(2,128)(2,1)} %bitcast.7), kind=kLoop, calls=%fused_computation.15 | loop fusion | bytes 1867780 | tf_op jit(solution)/shard_map/jit(dynamic_update_index_in_dim)/dynamic_update_slice | solution.py:38
  148.6 2.3 %copy_dynamic-update-slice_fusion.4 = bf16[4,8,2,36,768]{4,3,1,0,2:T(8,128)(2,1)} fusion(bf16[4,8,2,36,768]{4,3,1,0,2:T(8,128)(2,1)} %copy_dynamic-update-slice_fusion.5, s32[]{:T(128)S(6)} %max.11, bf16[1,8,2,36,768]{4,2,3,1,0:T(2,128)(2,1)} %bitcast.8), kind=kLoop, calls=%fused_computation.14 | loop fusion | bytes 1867780 | tf_op jit(solution)/shard_map/jit(dynamic_update_index_in_dim)/dynamic_update_slice | solution.py:38
  151.0 13.7 %collective-permute-done.5 = bf16[8,2,36,768]{3,1,2,0:T(2,128)(2,1)} collective-permute-done((bf16[8,2,36,768]{3,1,2,0:T(2,128)(2,1)}, bf16[8,2,36,768]{3,1,2,0:T(2,128)(2,1)}, u32[]{:S(2)}, u32[]{:S(2)}) %collective-permute-start.5) | collective-permute-done | bytes 884768 | tf_op jit(solution)/shard_map/ppermute | solution.py:33
  164.7 2.2 %copy_dynamic-update-slice_fusion.3 = bf16[4,8,2,36,768]{4,3,1,0,2:T(8,128)(2,1)} fusion(bf16[4,8,2,36,768]{4,3,1,0,2:T(8,128)(2,1)} %copy_dynamic-update-slice_fusion.4, s32[]{:T(128)S(6)} %select_n.93, bf16[1,8,2,36,768]{4,2,3,1,0:T(2,128)(2,1)} %bitcast.9), kind=kLoop, calls=%fused_computation.13 | loop fusion | bytes 1867780 | tf_op jit(solution)/shard_map/jit(dynamic_update_index_in_dim)/dynamic_update_slice | solution.py:42
  166.9 2.2 %copy_dynamic-update-slice_fusion.2 = bf16[4,8,2,36,768]{4,3,1,0,2:T(8,128)(2,1)} fusion(bf16[4,8,2,36,768]{4,3,1,0,2:T(8,128)(2,1)} %copy_dynamic-update-slice_fusion.3, s32[]{:T(128)S(6)} %select_n.94, bf16[1,8,2,36,768]{4,2,3,1,0:T(2,128)(2,1)} %bitcast.10), kind=kLoop, calls=%fused_computation.12 | loop fusion | bytes 1867780 | tf_op jit(solution)/shard_map/jit(dynamic_update_index_in_dim)/dynamic_update_slice | solution.py:42
  171.3 5.6 %fusion = f32[8,4,2,36]{3,0,1,2:T(8,128)S(1)} fusion(bf16[8,4,2,36,512]{4,1,3,2,0:T(4,128)(2,1)} %all-to-all-done, bf16[4,8,2,36,768]{4,3,1,0,2:T(8,128)(2,1)} %copy_dynamic-update-slice_fusion, bf16[2,768,512]{2,1,0:T(8,128)(2,1)S(1)} %copy-done), kind=kOutput, calls=%fused_computation.2 | convolution fusion | flops 1817835264 | bytes 7480320 | tf_op jit(solution)/shard_map/csekf,efn->scekn/dot_general | solution.py:57
  177.6 3.8 %all-to-all-start.1 = ((f32[8,1,288]{2,1,0:T(1,128)}), f32[8,1,288]{2,1,0:T(1,128)S(1)}, u32[]{:S(2)}, u32[]{:S(2)}) async-start(f32[8,1,288]{2,1,0:T(1,128)} %reshape.217), calls=%async_computation.1 | async-start | bytes 24576 | tf_op jit(solution)/shard_map/all_to_all | solution.py:61
  181.5 4.6 %all-to-all-done.1 = f32[8,1,288]{2,1,0:T(1,128)S(1)} async-done(((f32[8,1,288]{2,1,0:T(1,128)}), f32[8,1,288]{2,1,0:T(1,128)S(1)}, u32[]{:S(2)}, u32[]{:S(2)}) %all-to-all-start.1) | async-done | bytes 9248 | tf_op jit(solution)/shard_map/all_to_all | solution.py:61
  187.4 13.4 %all-gather.2 = f32[32,4,2,36]{3,1,2,0:T(4,128)S(1)} all-gather(f32[8,4,2,36]{3,1,2,0:T(4,128)S(1)} %bitcast.71), channel_id=4, replica_groups=mesh['ctx'=4,'exp'=8] {'ctx'}, dimensions={0}, use_global_device_ids=true | all-gather | bytes 46080 | tf_op jit(solution)/shard_map/all_gather | solution.py:64
  203.3 3.7 %add_convert_fusion = bf16[4,128,2048]{2,1,0:T(8,128)(2,1)S(1)} fusion(bf16[4,128,2048]{2,1,0:T(8,128)(2,1)} %bitcast.64, f32[4,128,16]{1,2,0:T(8,128)S(1)} %select_reduce_fusion.1, bf16[2048,16]{0,1:T(8,128)(2,1)S(1)} %copy-done.2), kind=kOutput, calls=%fused_computation.5 | convolution fusion | flops 204472320 | bytes 4292608 | tf_op jit(solution)/shard_map/dot_general | solution.py:79
  207.0 3.3 %convolution_convert_fusion = bf16[512,1024]{1,0:T(8,128)(2,1)} fusion(bf16[512,2048]{1,0:T(8,128)(2,1)S(1)} %bitcast.65, bf16[1024,2048]{1,0:T(8,128)(2,1)S(1)} %copy-done.3), kind=kOutput, calls=%fused_computation.7 | convolution fusion | flops 2148007936 | bytes 7340032 | tf_op jit(solution)/shard_map/dot_general | solution.py:83
  (59 shorter events, 18.6 us)
Async XLA Ops:
  7.2 164.1 %copy-start = (bf16[2,768,512]{2,1,0:T(8,128)(2,1)S(1)}, bf16[2,768,512]{2,1,0:T(8,128)(2,1)}, u32[]{:S(2)}) copy-start(bf16[2,768,512]{2,1,0:T(8,128)(2,1)} %param.11) | copy-start | bytes 4718596
  7.2 100.1 %all-gather.5.cloned.1.call-start = ((), (), s32[]{:S(2)}) async-start(), calls=%async_computation.2 | async-start | bytes 2621440 | tf_op jit(solution)/shard_map/all_gather | solution.py:24
  7.9 36.7 %collective-permute-start = (bf16[8,2,36,768]{3,1,2,0:T(2,128)(2,1)}, bf16[8,2,36,768]{3,1,2,0:T(2,128)(2,1)}, u32[]{:S(2)}, u32[]{:S(2)}) collective-permute-start(bf16[8,2,36,768]{3,1,2,0:T(2,128)(2,1)} %bitcast.66), channel_id=1, source_target_pairs={{0,8},{8,16},{16,24},{1,9},{9,17},{17,25},{2,10},{10,18},{18,26},{... | collective-permute-start | bytes 2654216 | tf_op jit(solution)/shard_map/ppermute | solution.py:32
  13.8 85.1 %collective-permute-start.3 = (bf16[8,2,36,768]{3,1,2,0:T(2,128)(2,1)}, bf16[8,2,36,768]{3,1,2,0:T(2,128)(2,1)S(1)}, u32[]{:S(2)}, u32[]{:S(2)}) collective-permute-start(bf16[8,2,36,768]{3,1,2,0:T(2,128)(2,1)} %bitcast.67), channel_id=1, source_target_pairs={{8,0},{16,8},{24,16},{9,1},{17,9},{25,17},{10,2},{18,10},{26,18},{... | collective-permute-start | bytes 2654216 | tf_op jit(solution)/shard_map/ppermute | solution.py:33
  44.6 55.6 %collective-permute-start.1 = (bf16[8,2,36,768]{3,1,2,0:T(2,128)(2,1)}, bf16[8,2,36,768]{3,1,2,0:T(2,128)(2,1)}, u32[]{:S(2)}, u32[]{:S(2)}) collective-permute-start(bf16[8,2,36,768]{3,1,2,0:T(2,128)(2,1)} %collective-permute-done), channel_id=1, source_target_pairs={{0,8},{8,16},{16,24},{1,9},{9,17},{17,25},{2,10},{10,18},{18,26},{... | collective-permute-start | bytes 2654216 | tf_op jit(solution)/shard_map/ppermute | solution.py:32
  99.0 41.6 %collective-permute-start.4 = (bf16[8,2,36,768]{3,1,2,0:T(2,128)(2,1)S(1)}, bf16[8,2,36,768]{3,1,2,0:T(2,128)(2,1)}, u32[]{:S(2)}, u32[]{:S(2)}) collective-permute-start(bf16[8,2,36,768]{3,1,2,0:T(2,128)(2,1)S(1)} %collective-permute-done.3), channel_id=1, source_target_pairs={{8,0},{16,8},{24,16},{9,1},{17,9},{25,17},{10,2},{18,10},{26,18},{... | collective-permute-start | bytes 2654216 | tf_op jit(solution)/shard_map/ppermute | solution.py:33
  100.3 41.8 %collective-permute-start.2 = (bf16[8,2,36,768]{3,1,2,0:T(2,128)(2,1)}, bf16[8,2,36,768]{3,1,2,0:T(2,128)(2,1)}, u32[]{:S(2)}, u32[]{:S(2)}) collective-permute-start(bf16[8,2,36,768]{3,1,2,0:T(2,128)(2,1)} %collective-permute-done.1), channel_id=1, source_target_pairs={{0,8},{8,16},{16,24},{1,9},{9,17},{17,25},{2,10},{10,18},{18,26},{... | collective-permute-start | bytes 2654216 | tf_op jit(solution)/shard_map/ppermute | solution.py:32
  136.1 35.1 %all-to-all-start = ((bf16[8,4,2,36,512]{4,1,3,2,0:T(4,128)(2,1)}), bf16[8,4,2,36,512]{4,1,3,2,0:T(4,128)(2,1)}, u32[]{:S(2)}, u32[]{:S(2)}) async-start(bf16[8,4,2,36,512]{4,1,3,2,0:T(4,128)(2,1)} %copy.82), calls=%async_computation | async-start | bytes 4718592 | tf_op jit(solution)/shard_map/all_to_all | solution.py:56
  140.5 24.1 %collective-permute-start.5 = (bf16[8,2,36,768]{3,1,2,0:T(2,128)(2,1)}, bf16[8,2,36,768]{3,1,2,0:T(2,128)(2,1)}, u32[]{:S(2)}, u32[]{:S(2)}) collective-permute-start(bf16[8,2,36,768]{3,1,2,0:T(2,128)(2,1)} %collective-permute-done.4), channel_id=1, source_target_pairs={{8,0},{16,8},{24,16},{9,1},{17,9},{25,17},{10,2},{18,10},{26,18},{... | collective-permute-start | bytes 2654216 | tf_op jit(solution)/shard_map/ppermute | solution.py:33
  148.6 21.5 %copy-start.1 = (bf16[1,8,2,36,768]{4,2,3,1,0:T(2,128)(2,1)S(1)}, bf16[1,8,2,36,768]{4,2,3,1,0:T(2,128)(2,1)}, u32[]{:S(2)}) copy-start(bf16[1,8,2,36,768]{4,2,3,1,0:T(2,128)(2,1)} %param.10) | copy-start | bytes 2654212
  171.2 32.0 %copy-start.2 = (bf16[2048,16]{0,1:T(8,128)(2,1)S(1)}, bf16[2048,16]{0,1:T(8,128)(2,1)}, u32[]{:S(2)}) copy-start(bf16[2048,16]{0,1:T(8,128)(2,1)} %param.12) | copy-start | bytes 196612
  177.6 8.6 %all-to-all-start.1 = ((f32[8,1,288]{2,1,0:T(1,128)}), f32[8,1,288]{2,1,0:T(1,128)S(1)}, u32[]{:S(2)}, u32[]{:S(2)}) async-start(f32[8,1,288]{2,1,0:T(1,128)} %reshape.217), calls=%async_computation.1 | async-start | bytes 24576 | tf_op jit(solution)/shard_map/all_to_all | solution.py:61
  203.3 3.7 %copy-start.3 = (bf16[1024,2048]{1,0:T(8,128)(2,1)S(1)}, bf16[1024,2048]{1,0:T(8,128)(2,1)}, u32[]{:S(2)}) copy-start(bf16[1024,2048]{1,0:T(8,128)(2,1)} %param.13) | copy-start | bytes 12582916
Sparse Core Ops, SparseCore 0:
  9.6 66.6 all-gather.4
